TPU v7x, 32 devices: a whole 2x2x4 slice. The times are simulated.
32 devices in a mesh: dp: 8 (over z, core), tensor: 4 (over y, x).
Axes of the slice: x: 2, y: 2, z: 4, core: 2. Of those that a mesh axis runs over, the one named last changes fastest.
Arguments:
- hidden: bfloat16 [4, 128, 8192], P(None, 'dp'), may hold values from -6 to 6
- queries: bfloat16 [4, 128, 8192], P(None, 'dp', 'tensor'), may hold values from -128 to 128
- projections: bfloat16 [2, 8192, 1024], P(None, ('dp', 'tensor')), may hold values from -0.0625 to 0.0625
- cache_keys: bfloat16 [128, 256, 1024], P('dp', None, 'tensor'), may hold values from -6 to 6, as said below
- cache_values: bfloat16 [128, 256, 1024], P('dp', None, 'tensor'), may hold values from -6 to 6
- lengths: int32 [128], P('dp'), may hold values from 2 to 252
- finished: int32 [128], P('dp'), may hold values from 0 to 1
- row_moves: int32 [128], P('dp'), may hold values from -1 to 1, as said below
Outputs:
- attention: bfloat16 [4, 128, 8192], P(None, 'dp', 'tensor')
- arrived_keys: bfloat16 [48, 256, 1024], P('dp', None, 'tensor')
- arrived_values: bfloat16 [48, 256, 1024], P('dp', None, 'tensor')
Inputs may be any that keep to these rules, and one draw needn't show every extreme that they name: `cache_keys`: cached keys of the model's attention. Within one data group's 16 rows at most 3 entries are 1 and at most 3 are -1; in every draw some group has exactly 3 rows with finished = 1 and row_moves = 1, and some group exactly 3 rows with finished = 1 and row_moves = -1.
All inputs are finite; a program needn't handle non-finite values.
Results may differ from a plain program's by a relative error of at most 0.0051.
Values may be sent and summed in bfloat16 or wider, within the bound.
A program may use at most 64 MiB of HBM per device.

v0:
```python
import jax
import jax.numpy as jnp
from jax import lax
from jax.sharding import PartitionSpec as P

HD = 128


def shifted(shard, axis, by):
    size = lax.axis_size(axis)
    return lax.ppermute(shard, axis, [(i, (i + by) % size) for i in range(size)])


def attend(query_block, new_keys, new_values, old_keys, old_values, row_lengths):
    step_count, row_count, query_width = query_block.shape
    cache_len = old_keys.shape[1]
    kv_heads = old_keys.shape[2] // HD
    group_size = query_width // (kv_heads * HD)
    inv_root = HD ** (-0.5)
    query_f = query_block.astype(jnp.float32).reshape(
        step_count, row_count, kv_heads, group_size, HD
    )
    cached_k = old_keys.astype(jnp.float32).reshape(row_count, cache_len, kv_heads, HD)
    cached_v = old_values.astype(jnp.float32).reshape(row_count, cache_len, kv_heads, HD)
    fresh_k = new_keys.astype(jnp.float32).reshape(step_count, row_count, kv_heads, HD)
    fresh_v = new_values.astype(jnp.float32).reshape(step_count, row_count, kv_heads, HD)
    score_old = jnp.einsum("trkgd,rpkd->trkgp", query_f, cached_k) * inv_root
    score_new = jnp.einsum("trkgd,srkd->trkgs", query_f, fresh_k) * inv_root
    positions = jnp.arange(cache_len, dtype=jnp.int32)
    valid_old = (positions[None, :] < row_lengths[:, None])[None, :, None, None, :]
    step_ids = jnp.arange(step_count, dtype=jnp.int32)
    valid_new = (step_ids[None, :] <= step_ids[:, None])[:, None, None, None, :]
    masked_out = jnp.float32(-1e30)
    score_old = jnp.where(valid_old, score_old, masked_out)
    score_new = jnp.where(valid_new, score_new, masked_out)
    highest = jnp.maximum(
        jnp.max(score_old, axis=-1, keepdims=True), jnp.max(score_new, axis=-1, keepdims=True)
    )
    expo_old = jnp.exp(score_old - highest)
    expo_new = jnp.exp(score_new - highest)
    totals = jnp.sum(expo_old, axis=-1, keepdims=True) + jnp.sum(expo_new, axis=-1, keepdims=True)
    weight_old = (expo_old / totals).astype(jnp.bfloat16)
    weight_new = (expo_new / totals).astype(jnp.bfloat16)
    output = jnp.einsum("trkgp,rpkd->trkgd", weight_old.astype(jnp.float32), cached_v)
    output = output + jnp.einsum("trkgs,srkd->trkgd", weight_new.astype(jnp.float32), fresh_v)
    return output.reshape(step_count, row_count, query_width).astype(jnp.bfloat16)


def write_new(old_cache, fresh, row_lengths):
    cache_len = old_cache.shape[1]
    positions = jnp.arange(cache_len, dtype=jnp.int32)
    result = old_cache
    for step_id in range(fresh.shape[0]):
        target = (positions[None, :] == (row_lengths + step_id)[:, None])[:, :, None]
        result = jnp.where(target, fresh[step_id][:, None, :], result)
    return result


def select_rows(final_cache, chosen, slot_count):
    row_count = final_cache.shape[0]
    ranks = jnp.cumsum(chosen) - 1
    slot_ids = jnp.arange(slot_count, dtype=jnp.int32)
    one_hot = ((ranks[None, :] == slot_ids[:, None]) & (chosen[None, :] == 1)).astype(jnp.bfloat16)
    picked = jnp.dot(
        one_hot, final_cache.reshape(row_count, -1), preferred_element_type=jnp.float32
    )
    return picked.astype(jnp.bfloat16).reshape((slot_count,) + final_cache.shape[1:])


def per_device(
    hidden, queries, projections, cache_keys, cache_values, lengths, finished, row_moves
):
    step_count, row_count, model_width = hidden.shape
    dp_count = lax.axis_size("dp")
    tensor_count = lax.axis_size("tensor")
    shard_rows = projections.shape[1]
    padded_width = dp_count * tensor_count * shard_rows
    token_count = step_count * row_count
    flat_rows = jnp.pad(
        hidden.reshape(token_count, model_width), ((0, 0), (0, padded_width - model_width))
    )
    local_width = cache_keys.shape[2]
    regrouped = lax.all_to_all(projections, "tensor", split_axis=2, concat_axis=1, tiled=True)
    portion = lax.all_gather(regrouped, "dp", axis=1, tiled=True)
    key_sum = jnp.dot(flat_rows, portion[0], preferred_element_type=jnp.float32)
    value_sum = jnp.dot(flat_rows, portion[1], preferred_element_type=jnp.float32)
    new_keys = key_sum.astype(jnp.bfloat16).reshape(step_count, row_count, local_width)
    new_values = value_sum.astype(jnp.bfloat16).reshape(step_count, row_count, local_width)
    attention = attend(queries, new_keys, new_values, cache_keys, cache_values, lengths)
    final_keys = write_new(cache_keys, new_keys, lengths)
    final_values = write_new(cache_values, new_values, lengths)
    slot_count = max(2, row_count // 5)
    going_up = ((finished == 1) & (row_moves == 1)).astype(jnp.int32)
    going_down = ((finished == 1) & (row_moves == -1)).astype(jnp.int32)
    up_keys = select_rows(final_keys, going_up, slot_count)
    up_values = select_rows(final_values, going_up, slot_count)
    down_keys = select_rows(final_keys, going_down, slot_count)
    down_values = select_rows(final_values, going_down, slot_count)
    from_before = shifted((up_keys, up_values), "dp", 1)
    from_after = shifted((down_keys, down_values), "dp", -1)
    arrived_keys = jnp.concatenate([from_before[0], from_after[0]], axis=0)
    arrived_values = jnp.concatenate([from_before[1], from_after[1]], axis=0)
    return (attention, arrived_keys, arrived_values)


def solution(mesh):
    in_specs = (
        P(None, "dp", None),
        P(None, "dp", "tensor"),
        P(None, ("dp", "tensor"), None),
        P("dp", None, "tensor"),
        P("dp", None, "tensor"),
        P("dp"),
        P("dp"),
        P("dp"),
    )
    out_specs = (P(None, "dp", "tensor"), P("dp", None, "tensor"), P("dp", None, "tensor"))
    return jax.shard_map(
        per_device, mesh=mesh, in_specs=in_specs, out_specs=out_specs, check_vma=False
    )
```

profile of v0, /device:TPU:0, one launch (start us, length us, event | category | flops | bytes accessed | tf_op | source)
XLA Modules:
  0.0 156.3 jit_solution(14865890176840857726)
XLA Ops:
  7.2 2.6 %copy.41 = bf16[2,256,1024]{1,0,2:T(2,128)(2,1)S(1)} copy(bf16[2,256,1024]{2,1,0:T(8,128)(2,1)} %param.10) | data formatting | bytes 2097152 | tf_op args[2]
  9.8 19.1 %all_to_all.18 = bf16[2,256,1024]{1,0,2:T(2,128)(2,1)S(1)} all-to-all(bf16[2,256,1024]{1,0,2:T(2,128)(2,1)S(1)} %copy.41), channel_id=1, replica_groups=mesh['dp'=8,'tensor'=4] {'tensor'}, dimensions={2} | all-to-all | bytes 2097152 | tf_op jit(solution)/shard_map/all_to_all | solution.py:83
  29.0 0.1 copy.42
  29.1 1.3 copy.43
  30.8 4.2 %reshape.255 = bf16[16,256,2,128]{3,2,1,0:T(2,128)(2,1)} reshape(bf16[16,256,256]{2,1,0:T(8,128)(2,1)} %param.11) | data formatting | bytes 4194304 | tf_op jit(solution)/shard_map/reshape | solution.py:23
  35.0 2.1 %reshape.259 = bf16[16,256,2,128]{3,2,1,0:T(2,128)(2,1)} reshape(bf16[16,256,256]{2,1,0:T(8,128)(2,1)S(1)} %copy-done.1) | data formatting | bytes 4194304 | tf_op jit(solution)/shard_map/reshape | solution.py:24
  37.0 0.1 add_reduce_fusion.1
  37.5 4.3 %fusion.52 = (f32[4,16,2,8]{3,0,2,1:T(4,128)}, f32[4,16,2,8,256]{4,3,0,2,1:T(8,128)}) fusion(bf16[4,16,2,8,128]{4,3,2,1,0:T(8,128)(2,1)S(1)} %bitcast.90, bf16[16,256,2,128,1]{3,2,1,0,4:T(2,128)(2,1)} %bitcast.84, pred[16,256]{1,0:T(8,128)(4,1)S(1)} %get-tuple-element.21), kind=kOutput, calls=%fused_computation.77 | convolution fusion | flops 67894272 | bytes 3416064 | tf_op jit(solution)/shard_map/trkgd,rpkd->trkgp/dot_general | solution.py:27
  41.8 70.5 %all-gather.2.cloned.1.call-done = bf16[2,8192,256]{2,1,0:T(8,128)(2,1)} async-done(((bf16[2,1024,256]{2,1,0:T(8,128)(2,1)}), bf16[2,8192,256]{2,1,0:T(8,128)(2,1)}) %all-gather.2.cloned.1.call-update) | async-done | bytes 8388624 | tf_op jit(solution)/shard_map/all_gather | solution.py:84
  112.4 3.0 %fusion.22 = bf16[64,256]{1,0:T(8,128)(2,1)S(1)} fusion(bf16[64,8192]{1,0:T(8,128)(2,1)S(1)} %bitcast.69, bf16[2,8192,256]{2,1,0:T(8,128)(2,1)} %all-gather.2.cloned.1.call-done), kind=kOutput, calls=%fused_computation.24 | convolution fusion | flops 268451840 | bytes 5275648 | tf_op jit(solution)/shard_map/dot_general | solution.py:85
  115.4 3.1 %fusion.23 = bf16[64,256]{1,0:T(8,128)(2,1)S(1)} fusion(bf16[64,8192]{1,0:T(8,128)(2,1)S(1)} %bitcast.70, bf16[2,8192,256]{2,1,0:T(8,128)(2,1)} %all-gather.2.cloned.1.call-done), kind=kOutput, calls=%fused_computation.25 | convolution fusion | flops 268451840 | bytes 5275648 | tf_op jit(solution)/shard_map/dot_general | solution.py:86
  118.5 2.8 %select_select_fusion = (bf16[16,256,256]{2,1,0:T(8,128)(2,1)S(1)}, bf16[16,256,256]{2,1,0:T(8,128)(2,1)S(1)}) fusion(bf16[16,256,256]{2,1,0:T(8,128)(2,1)S(1)} %copy-done.1, pred[16,256]{1,0:T(8,128)(4,1)S(1)} %get-tuple-element.20, pred[16,256]{1,0:T(8,128)(4,1)S(1)} %get-tuple-element.26, pred[16,256]{1,0:T(8,128)(4,1)S(1)} %get-tuple-element.27, ...), kind=kLoop, calls=%fused_computation.12 | loop fusion | flops 8388608 | bytes 8470528 | tf_op jit(solution)/shard_map/jit(_where)/select_n | solution.py:55
  121.4 1.2 copy.67
  122.6 1.2 copy.64
  123.8 0.4 convolution_convert_fusion.1
  124.2 0.4 convolution_convert_fusion.3
  124.7 0.4 convolution_convert_fusion
  125.1 0.4 convolution_convert_fusion.2
  125.6 0.6 reshape.258
  126.3 0.3 collective-permute-start.2
  126.6 3.4 %collective-permute-start.3 = (bf16[3,256,256]{2,1,0:T(8,128)(2,1)S(1)}, bf16[3,256,256]{2,1,0:T(8,128)(2,1)}, u32[]{:S(2)}, u32[]{:S(2)}) collective-permute-start(bf16[3,256,256]{2,1,0:T(8,128)(2,1)S(1)} %bitcast.87), channel_id=1, source_target_pairs={{0,28},{4,0},{8,4},{12,8},{16,12},{20,16},{24,20},{28,24},{1,29},{... | collective-permute-start | bytes 1179656 | tf_op jit(solution)/shard_map/ppermute | solution.py:11
  130.2 3.6 %collective-permute-start.1 = (bf16[3,256,256]{2,1,0:T(8,128)(2,1)S(1)}, bf16[3,256,256]{2,1,0:T(8,128)(2,1)}, u32[]{:S(2)}, u32[]{:S(2)}) collective-permute-start(bf16[3,256,256]{2,1,0:T(8,128)(2,1)S(1)} %bitcast.88), channel_id=1, source_target_pairs={{0,28},{4,0},{8,4},{12,8},{16,12},{20,16},{24,20},{28,24},{1,29},{... | collective-permute-start | bytes 1179656 | tf_op jit(solution)/shard_map/ppermute | solution.py:11
  133.8 1.3 fusion.53
  135.1 0.3 fusion.29
  135.4 0.5 fusion.24
  135.9 1.3 fusion.15
  137.2 1.4 fusion.19
  138.7 0.8 convert_element_type.52
  139.5 0.1 collective-permute-done.2
  139.7 2.1 %pad_maximum_fusion.1 = bf16[6,256,256]{2,1,0:T(8,128)(2,1)} fusion(bf16[3,256,256]{2,1,0:T(8,128)(2,1)} %collective-permute-done.3, bf16[3,256,256]{2,1,0:T(8,128)(2,1)} %collective-permute-done.2), kind=kLoop, calls=%fused_computation.30 | loop fusion | flops 393216 | bytes 1572864 | tf_op jit(solution)/shard_map/concatenate | solution.py:102
  141.7 5.6 %collective-permute-done = bf16[3,256,256]{2,1,0:T(8,128)(2,1)} collective-permute-done((bf16[3,256,256]{2,1,0:T(8,128)(2,1)S(1)}, bf16[3,256,256]{2,1,0:T(8,128)(2,1)}, u32[]{:S(2)}, u32[]{:S(2)}) %collective-permute-start) | collective-permute-done | bytes 393248 | tf_op jit(solution)/shard_map/ppermute | solution.py:11
  147.4 2.1 %pad_maximum_fusion = bf16[6,256,256]{2,1,0:T(8,128)(2,1)} fusion(bf16[3,256,256]{2,1,0:T(8,128)(2,1)} %collective-permute-done.1, bf16[3,256,256]{2,1,0:T(8,128)(2,1)} %collective-permute-done), kind=kLoop, calls=%fused_computation.29 | loop fusion | flops 393216 | bytes 1572864 | tf_op jit(solution)/shard_map/concatenate | solution.py:101
  (56 shorter events, 1.2 us)
Async XLA Ops:
  7.2 105.2 %copy-start = (bf16[4,16,8192]{2,1,0:T(8,128)(2,1)S(1)}, bf16[4,16,8192]{2,1,0:T(8,128)(2,1)}, u32[]{:S(2)}) copy-start(bf16[4,16,8192]{2,1,0:T(8,128)(2,1)} %param.8) | copy-start | bytes 3145732
  7.2 105.2 %all-gather.2.cloned.1.call-start = ((), (), s32[]{:S(2)}) async-start(), calls=%async_computation.1 | async-start | bytes 9437184 | tf_op jit(solution)/shard_map/all_gather | solution.py:84
  29.1 1.4 copy-start.13
  29.1 1.4 copy-start.14
  29.1 1.6 %copy-start.5 = (bf16[4,16,2048]{2,1,0:T(8,128)(2,1)S(1)}, bf16[4,16,2048]{2,1,0:T(8,128)(2,1)}, u32[]{:S(2)}) copy-start(bf16[4,16,2048]{2,1,0:T(8,128)(2,1)} %param.9) | copy-start | bytes 786436
  30.8 6.8 %copy-start.6 = (bf16[8,8,16,128]{3,2,1,0:T(8,128)(2,1)}, bf16[8,8,16,128]{3,2,1,0:T(8,128)(2,1)S(1)}, u32[]{:S(2)}) copy-start(bf16[8,8,16,128]{3,2,1,0:T(8,128)(2,1)S(1)} %copy.63) | copy-start | bytes 786436
  30.8 4.2 %copy-start.1 = (bf16[16,256,256]{2,1,0:T(8,128)(2,1)S(1)}, bf16[16,256,256]{2,1,0:T(8,128)(2,1)}, u32[]{:S(2)}) copy-start(bf16[16,256,256]{2,1,0:T(8,128)(2,1)} %param.12) | copy-start | bytes 6291460
  35.0 2.3 %copy-start.12 = (s32[16]{0:T(128)S(1)}, s32[16]{0:T(128)}, u32[]{:S(2)}) copy-start(s32[16]{0:T(128)} %param.13) | copy-start | bytes 196
  115.4 3.2 %copy-start.2 = (bf16[16,256,256]{2,1,0:T(8,128)(2,1)S(1)}, bf16[16,256,256]{2,1,0:T(8,128)(2,1)}, u32[]{:S(2)}) copy-start(bf16[16,256,256]{2,1,0:T(8,128)(2,1)} %param.11) | copy-start | bytes 6291460
  118.5 2.9 %copy-start.8 = (bf16[64,256]{1,0:T(8,128)(2,1)}, bf16[64,256]{1,0:T(8,128)(2,1)S(1)}, u32[]{:S(2)}) copy-start(bf16[64,256]{1,0:T(8,128)(2,1)S(1)} %fusion.23) | copy-start | bytes 98308
  126.2 7.5 %copy-start.7 = (bf16[8,8,16,128]{3,2,1,0:T(8,128)(2,1)S(1)}, bf16[8,8,16,128]{3,2,1,0:T(8,128)(2,1)}, u32[]{:S(2)}) copy-start(bf16[8,8,16,128]{3,2,1,0:T(8,128)(2,1)} %copy-done.6) | copy-start | bytes 786436
  126.2 7.5 %copy-start.11 = (bf16[4,16,2,128]{3,2,1,0:T(2,128)(2,1)S(1)}, bf16[4,16,2,128]{3,2,1,0:T(2,128)(2,1)}, u32[]{:S(2)}) copy-start(bf16[4,16,2,128]{3,2,1,0:T(2,128)(2,1)} %reshape.258) | copy-start | bytes 98308
  126.2 8.8 %copy-start.10 = (f32[4,16,2,8]{3,0,2,1:T(4,128)S(1)}, f32[4,16,2,8]{3,0,2,1:T(4,128)}, u32[]{:S(2)}) copy-start(f32[4,16,2,8]{3,0,2,1:T(4,128)} %get-tuple-element.22) | copy-start | bytes 12292
  126.3 13.4 %collective-permute-start.2 = (bf16[3,256,256]{2,1,0:T(8,128)(2,1)S(1)}, bf16[3,256,256]{2,1,0:T(8,128)(2,1)}, u32[]{:S(2)}, u32[]{:S(2)}) collective-permute-start(bf16[3,256,256]{2,1,0:T(8,128)(2,1)S(1)} %bitcast.85), channel_id=1, source_target_pairs={{0,4},{4,8},{8,12},{12,16},{16,20},{20,24},{24,28},{28,0},{1,5},{5... | collective-permute-start | bytes 1179656 | tf_op jit(solution)/shard_map/ppermute | solution.py:11
  126.6 8.8 %copy-start.4 = (f32[4,16,2,8,256]{4,3,0,2,1:T(8,128)S(1)}, f32[4,16,2,8,256]{4,3,0,2,1:T(8,128)}, u32[]{:S(2)}) copy-start(f32[4,16,2,8,256]{4,3,0,2,1:T(8,128)} %get-tuple-element.23) | copy-start | bytes 3145732
  126.6 13.0 %collective-permute-start.3 = (bf16[3,256,256]{2,1,0:T(8,128)(2,1)S(1)}, bf16[3,256,256]{2,1,0:T(8,128)(2,1)}, u32[]{:S(2)}, u32[]{:S(2)}) collective-permute-start(bf16[3,256,256]{2,1,0:T(8,128)(2,1)S(1)} %bitcast.87), channel_id=1, source_target_pairs={{0,28},{4,0},{8,4},{12,8},{16,12},{20,16},{24,20},{28,24},{1,29},{... | collective-permute-start | bytes 1179656 | tf_op jit(solution)/shard_map/ppermute | solution.py:11
  130.1 5.8 %copy-start.3 = (bf16[16,256,2,128]{3,2,1,0:T(2,128)(2,1)S(1)}, bf16[16,256,2,128]{3,2,1,0:T(2,128)(2,1)}, u32[]{:S(2)}) copy-start(bf16[16,256,2,128]{3,2,1,0:T(2,128)(2,1)} %reshape.259) | copy-start | bytes 6291460
  130.1 17.3 %collective-permute-start = (bf16[3,256,256]{2,1,0:T(8,128)(2,1)S(1)}, bf16[3,256,256]{2,1,0:T(8,128)(2,1)}, u32[]{:S(2)}, u32[]{:S(2)}) collective-permute-start(bf16[3,256,256]{2,1,0:T(8,128)(2,1)S(1)} %bitcast.86), channel_id=1, source_target_pairs={{0,4},{4,8},{8,12},{12,16},{16,20},{20,24},{24,28},{28,0},{1,5},{5... | collective-permute-start | bytes 1179656 | tf_op jit(solution)/shard_map/ppermute | solution.py:11
  130.2 17.2 %collective-permute-start.1 = (bf16[3,256,256]{2,1,0:T(8,128)(2,1)S(1)}, bf16[3,256,256]{2,1,0:T(8,128)(2,1)}, u32[]{:S(2)}, u32[]{:S(2)}) collective-permute-start(bf16[3,256,256]{2,1,0:T(8,128)(2,1)S(1)} %bitcast.88), channel_id=1, source_target_pairs={{0,28},{4,0},{8,4},{12,8},{16,12},{20,16},{24,20},{28,24},{1,29},{... | collective-permute-start | bytes 1179656 | tf_op jit(solution)/shard_map/ppermute | solution.py:11
  135.9 1.4 copy-start.9
Sparse Core Ops, SparseCore 0:
  30.6 81.7 all-gather.1
where the time goes:
time: 157 us; the launch traced here: 156 us
  waiting for transfers between devices  76.4 us (49%)
  blocking collectives  19.1 us (12%)
  matrix products  16.2 us (10%)
  local copies, waits for them, and re-layouts  14.7 us (9%)
  between operations  14.3 us (9%)
  other arithmetic  8.26 us (5%)
  starting transfers between devices  7.32 us (5%)
    all_gather x1, waiting for transfers between devices, per_device(): portion = lax.all_gather(regrouped, 'dp', axis=1, tiled=True)  70.5 us
    all_to_all x1, blocking collectives, per_device(): lax.all_to_all(projections, 'tensor', split_axis=2, concat_axis=1, tiled=...  19.1 us
    ppermute x4, starting transfers between devices, shifted(): lax.ppermute(shard, axis, [(i, (i + by) % size) for i in range(size)])  7.28 us
    ppermute x4, waiting for transfers between devices, shifted(): lax.ppermute(shard, axis, [(i, (i + by) % size) for i in range(size)])  5.8 us
    unnamed x38, local copies, waits for them, and re-layouts  5.31 us
    dot_general x1, matrix products, attend(): score_old = jnp.einsum('trkgd,rpkd->trkgp', query_f, cached_k) * inv_root  4.29 us
    reshape x1, local copies, waits for them, and re-layouts, attend(): old_keys.astype(jnp.float32).reshape(row_count, cache_len, kv_heads, HD)  4.16 us
  transfers between devices with their start and end apart: 5, of which 3 were waited for; matrix products, arithmetic and copies ran while one was open for 12% of the time, Pallas kernels for 0%

commit v1 on v0

--- a/solution.py
+++ b/solution.py
@@ -1,9 +1,15 @@
+import functools
+
 import jax
 import jax.numpy as jnp
 from jax import lax
+from jax.experimental import pallas as pl
+from jax.experimental.pallas import tpu as pltpu
 from jax.sharding import PartitionSpec as P
 
 HD = 128
+PAD = 8
+MESH = pl.DeviceIdType.MESH
 
 
 def shifted(shard, axis, by):
@@ -103,6 +109,427 @@
     return (attention, arrived_keys, arrived_values)
 
 
+def fits_kernel(mesh, hidden, queries, projections, cache_keys, *_):
+    dp_count, tensor_count = mesh.shape["dp"], mesh.shape["tensor"]
+    step_count, rows_all, model_width = hidden.shape
+    row_count = rows_all // dp_count
+    shard_rows = projections.shape[1] // (dp_count * tensor_count)
+    local_width = cache_keys.shape[2] // tensor_count
+    return (
+        dp_count % 2 == 0
+        and 4 <= dp_count <= 16
+        and tensor_count <= 8
+        and projections.shape[1] == model_width
+        and shard_rows % 128 == 0
+        and row_count % 16 == 0
+        and local_width % HD == 0
+        and step_count < PAD
+        and cache_keys.shape[1] % 128 == 0
+    )
+
+
+def layer_kernel(
+    dp_count,
+    tensor_count,
+    slot_count,
+    lengths,
+    finished,
+    moves,
+    hidden,
+    queries,
+    projections,
+    cache_keys,
+    cache_values,
+    attention,
+    arrived_keys,
+    arrived_values,
+    hid,
+    wts,
+    cache,
+    qry,
+    q_rows,
+    expo,
+    top,
+    tot,
+    part,
+    mate_part,
+    joined,
+    far_part,
+    fresh,
+    staged,
+    landed,
+    news,
+    news_in,
+    out_rows,
+    local_sem,
+    hid_send,
+    hid_recv,
+    wt_send,
+    wt_recv,
+    move_send,
+    move_recv,
+    mate_send,
+    mate_recv,
+    far_send,
+    far_recv,
+    news_send,
+    news_recv,
+):
+    step_count, row_count, _ = hidden.shape
+    shard_rows, local_width = projections.shape[1], cache_keys.shape[2]
+    cache_len = cache_keys.shape[1]
+    depth = shard_rows * tensor_count
+    kv_heads = local_width // HD
+    group = queries.shape[2] // local_width
+    span = step_count * group
+    tokens = step_count * row_count
+    chips = dp_count // 2
+    me = lax.axis_index("dp")
+    col = lax.axis_index("tensor")
+    chip, core = me // 2, me % 2
+    mate = chip * 2 + 1 - core
+
+    def remote(src, dst, send, recv, dp_to, col_to=None):
+        return pltpu.make_async_remote_copy(
+            src_ref=src,
+            dst_ref=dst,
+            send_sem=send,
+            recv_sem=recv,
+            device_id=(dp_to, col if col_to is None else col_to),
+            device_id_type=MESH,
+        )
+
+    load_keys = pltpu.make_async_copy(cache_keys, cache.at[0], local_sem.at[0])
+    load_values = pltpu.make_async_copy(cache_values, cache.at[1], local_sem.at[1])
+    load_queries = pltpu.make_async_copy(queries, qry, local_sem.at[2])
+    own_hidden = pltpu.make_async_copy(
+        hidden.at[:, :, pl.ds(pl.multiple_of(me * depth, 128), depth)], hid.at[me], local_sem.at[3]
+    )
+    own_weights = pltpu.make_async_copy(
+        projections.at[:, :, pl.ds(pl.multiple_of(col * local_width, 128), local_width)],
+        wts.at[:, pl.ds(pl.multiple_of(col * shard_rows, 128), shard_rows), :],
+        local_sem.at[4],
+    )
+    for copy in (load_keys, load_values, load_queries, own_hidden, own_weights):
+        copy.start()
+
+    barrier = pltpu.get_barrier_semaphore()
+    for off in range(1, dp_count):
+        pl.semaphore_signal(
+            barrier, inc=1, device_id=((me + off) % dp_count, col), device_id_type=MESH
+        )
+    for off in range(1, tensor_count):
+        pl.semaphore_signal(
+            barrier, inc=1, device_id=(me, (col + off) % tensor_count), device_id_type=MESH
+        )
+    pl.semaphore_wait(barrier, dp_count + tensor_count - 2)
+
+    far_first = sorted(range(1, chips), key=lambda d: -min(d, chips - d))
+    hid_copies = []
+    for d in far_first + [0]:
+        for to_core in range(2):
+            if d == 0 and to_core == 1:
+                continue
+            to = ((chip + d) % chips) * 2 + to_core if d else mate
+            copy = remote(
+                hidden.at[:, :, pl.ds(pl.multiple_of(to * depth, 128), depth)],
+                hid.at[me],
+                hid_send.at[d, to_core],
+                hid_recv.at[d, core],
+                to,
+            )
+            copy.start()
+            hid_copies.append(copy)
+    wt_copies = []
+    for off in range(1, tensor_count):
+        to = (col + off) % tensor_count
+        copy = remote(
+            projections.at[:, :, pl.ds(pl.multiple_of(to * local_width, 128), local_width)],
+            wts.at[:, pl.ds(pl.multiple_of(col * shard_rows, 128), shard_rows), :],
+            wt_send.at[off],
+            wt_recv.at[off],
+            me,
+            to,
+        )
+        copy.start()
+        wt_copies.append(copy)
+
+    picks = []
+    for sign in (1, -1):
+        count = jnp.int32(0)
+        index = [jnp.int32(-1)] * slot_count
+        place = [jnp.int32(-1000)] * slot_count
+        for r in range(row_count):
+            leaves = ((finished[r] == 1) & (moves[r] == sign)).astype(jnp.int32)
+            for s in range(slot_count):
+                hit = leaves * (count == s).astype(jnp.int32)
+                index[s] = index[s] + hit * (r + 1)
+                place[s] = place[s] + hit * (lengths[r] + 1000)
+            count = count + leaves
+        picks.append((index, place))
+
+    load_keys.wait()
+    load_values.wait()
+    lot = 64
+    lots = cache_len // lot
+
+    def stage(step, carry):
+        kv, at = step // lots, pl.multiple_of((step % lots) * lot, lot)
+        blocks = [jnp.zeros((lot, local_width), cache.dtype)] * (2 * slot_count)
+        marks = [
+            jnp.full((lot, local_width), mark, jnp.int32).astype(jnp.float32).astype(cache.dtype)
+            for index, _ in picks
+            for mark in index
+        ]
+        for r in range(row_count):
+            row = cache[kv, r, pl.ds(at, lot), :]
+            blocks = [jnp.where(m == r, row, block) for m, block in zip(marks, blocks)]
+        for n, block in enumerate(blocks):
+            staged[n // slot_count, kv, n % slot_count, pl.ds(at, lot), :] = block
+        return carry
+
+    lax.fori_loop(0, 2 * lots, stage, 0)
+    load_queries.wait()
+    for t in range(step_count):
+        for k in range(kv_heads):
+            for g in range(group):
+                lane = (k * group + g) * HD
+                q_rows[k, pl.ds(t * group + g, row_count, stride=span), :] = qry[
+                    t, :, lane : lane + HD
+                ].astype(jnp.float32)
+    fresh[...] = jnp.zeros_like(fresh)
+
+    move_copies = []
+    for way in range(2):
+        to = (me + (1 if way == 0 else dp_count - 1)) % dp_count
+        copy = remote(staged.at[way], landed.at[way], move_send.at[way], move_recv.at[way], to)
+        copy.start()
+        move_copies.append(copy)
+
+    inv_root = HD ** (-0.5)
+    masked_out = jnp.float32(-1e30)
+
+    def old_scores(r, carry):
+        positions = lax.broadcasted_iota(jnp.int32, (span, cache_len), 1)
+        valid = positions < lengths[r]
+        rows = pl.ds(pl.multiple_of(r * span, 8), span)
+        for k in range(kv_heads):
+            score = lax.dot_general(
+                q_rows[k, rows, :].astype(jnp.bfloat16),
+                cache[0, r, :, k * HD : (k + 1) * HD],
+                (((1,), (1,)), ((), ())),
+                preferred_element_type=jnp.float32,
+            )
+            score = jnp.where(valid, score * inv_root, masked_out)
+            high = jnp.max(score, axis=1, keepdims=True)
+            raised = jnp.exp(score - high)
+            expo[k, rows, :] = raised
+            top[k, rows, :] = jnp.broadcast_to(high, (span, HD))
+            tot[k, rows, :] = jnp.broadcast_to(jnp.sum(raised, axis=1, keepdims=True), (span, HD))
+        return carry
+
+    lax.fori_loop(0, row_count, old_scores, 0, unroll=4)
+
+    own_hidden.wait()
+    own_weights.wait()
+    for off in range(1, tensor_count):
+        source = (col + tensor_count - off) % tensor_count
+        block = wts.at[:, pl.ds(pl.multiple_of(source * shard_rows, 128), shard_rows), :]
+        remote(block, block, wt_send.at[off], wt_recv.at[off], me, source).wait_recv()
+    near_first = [0] + far_first[::-1]
+    mate_copies = [None] * chips
+    for d in near_first:
+        source_chip = (chip + d) % chips
+        back = (chips - d) % chips
+        for from_core in range(2):
+            if d:
+                source = source_chip * 2 + from_core
+                block = hid.at[source]
+                remote(
+                    block, block, hid_send.at[back, from_core], hid_recv.at[back, from_core], source
+                ).wait_recv()
+        if d == 0:
+            block = hid.at[mate]
+            remote(block, block, hid_send.at[0, 0], hid_recv.at[0, 1 - core], mate).wait_recv()
+        states = hid[pl.ds(source_chip * 2, 2)].reshape(2 * tokens, depth)
+        for kv in range(2):
+            product = jnp.dot(states, wts[kv], preferred_element_type=jnp.float32)
+            part[d, :, kv] = product.reshape(2, tokens, local_width)
+        copy = remote(
+            part.at[d, 1 - core], mate_part.at[d], mate_send.at[d], mate_recv.at[d], mate
+        )
+        copy.start()
+        mate_copies[d] = copy
+    far_copies = []
+    for d in near_first[1:] + [0]:
+        mate_copies[d].wait_recv()
+        joined[d] = part[d, core] + mate_part[d]
+        if d:
+            copy = remote(
+                joined.at[d],
+                far_part.at[d],
+                far_send.at[d],
+                far_recv.at[d],
+                ((chip + d) % chips) * 2 + core,
+            )
+            copy.start()
+            far_copies.append(copy)
+    for copy in far_copies:
+        copy.wait_recv()
+    for kv in range(2):
+        total = joined[0, kv]
+        for d in range(1, chips):
+            total = total + far_part[d, kv]
+        total = total.astype(jnp.bfloat16).astype(jnp.float32)
+        for k in range(kv_heads):
+            for t in range(step_count):
+                fresh[kv, k, pl.ds(t, row_count, stride=PAD), :] = total[
+                    t * row_count : (t + 1) * row_count, k * HD : (k + 1) * HD
+                ]
+
+    news_copies = []
+    for way in range(2):
+        for s in range(slot_count):
+            mark = jnp.full((PAD, HD), picks[way][0][s], jnp.int32)
+            place = jnp.full((PAD, HD), picks[way][1][s], jnp.int32).astype(jnp.float32)
+            line = lax.broadcasted_iota(jnp.int32, (PAD, HD), 0)
+            for kv in range(2):
+                for k in range(kv_heads):
+                    rows = jnp.zeros((PAD, HD), jnp.float32)
+                    for r in range(row_count):
+                        rows = jnp.where(mark == r, fresh[kv, k, r * PAD : (r + 1) * PAD, :], rows)
+                    news[way, s, kv, :, k * HD : (k + 1) * HD] = jnp.where(
+                        line == step_count, place, rows
+                    )
+    for way in range(2):
+        to = (me + (1 if way == 0 else dp_count - 1)) % dp_count
+        copy = remote(news.at[way], news_in.at[way], news_send.at[way], news_recv.at[way], to)
+        copy.start()
+        news_copies.append(copy)
+
+    wide = (row_count * span, row_count * PAD)
+    row_of = lax.broadcasted_iota(jnp.int32, wide, 0)
+    new_of = lax.broadcasted_iota(jnp.int32, wide, 1)
+    seen = (row_of // span == new_of // PAD) & (new_of % PAD <= (row_of % span) // group)
+    for k in range(kv_heads):
+        score = lax.dot_general(
+            q_rows[k].astype(jnp.bfloat16),
+            fresh[0, k].astype(jnp.bfloat16),
+            (((1,), (1,)), ((), ())),
+            preferred_element_type=jnp.float32,
+        )
+        score = jnp.where(seen, score * inv_root, masked_out)
+        before = top[k][:, :1]
+        high = jnp.maximum(before, jnp.max(score, axis=1, keepdims=True))
+        raised = jnp.exp(score - high)
+        shrink = jnp.exp(before - high)
+        total = shrink * tot[k][:, :1] + jnp.sum(raised, axis=1, keepdims=True)
+        weight = (raised / total).astype(jnp.bfloat16)
+        out_rows[k] = jnp.dot(
+            weight, fresh[1, k].astype(jnp.bfloat16), preferred_element_type=jnp.float32
+        )
+        top[k] = jnp.broadcast_to(shrink / total, (row_count * span, HD))
+
+    def old_values(r, carry):
+        rows = pl.ds(pl.multiple_of(r * span, 8), span)
+        for k in range(kv_heads):
+            weight = (expo[k, rows, :] * top[k, rows, :][:, :1]).astype(jnp.bfloat16)
+            out_rows[k, rows, :] += jnp.dot(
+                weight,
+                cache[1, r, :, k * HD : (k + 1) * HD],
+                preferred_element_type=jnp.float32,
+            )
+        return carry
+
+    lax.fori_loop(0, row_count, old_values, 0, unroll=4)
+    for t in range(step_count):
+        for k in range(kv_heads):
+            for g in range(group):
+                lane = (k * group + g) * HD
+                attention[t, :, lane : lane + HD] = out_rows[
+                    k, pl.ds(t * group + g, row_count, stride=span), :
+                ].astype(attention.dtype)
+
+    for copy in move_copies + news_copies:
+        copy.wait_recv()
+    line = lax.broadcasted_iota(jnp.int32, (cache_len, local_width), 0).astype(jnp.float32)
+    for way in range(2):
+        for s in range(slot_count):
+            for kv, arrived in enumerate((arrived_keys, arrived_values)):
+                rows = news_in[way, s, kv]
+                ahead = line - rows[step_count : step_count + 1]
+                block = landed[way, kv, s].astype(jnp.float32)
+                for t in range(step_count):
+                    block = jnp.where(ahead == t, rows[t : t + 1], block)
+                arrived[way * slot_count + s] = block.astype(arrived.dtype)
+
+    for copy in hid_copies + wt_copies + move_copies + mate_copies + far_copies + news_copies:
+        copy.wait_send()
+
+
+def per_device_kernel(
+    hidden, queries, projections, cache_keys, cache_values, lengths, finished, row_moves
+):
+    dp_count = lax.axis_size("dp")
+    tensor_count = lax.axis_size("tensor")
+    step_count, row_count, _ = hidden.shape
+    _, cache_len, local_width = cache_keys.shape
+    slot_count = max(2, row_count // 5)
+    depth = projections.shape[1] * tensor_count
+    kv_heads = local_width // HD
+    span = step_count * (queries.shape[2] // local_width)
+    tokens = step_count * row_count
+    chips = dp_count // 2
+    kind = cache_keys.dtype
+    lines = row_count * span
+    arrived = jax.ShapeDtypeStruct((2 * slot_count, cache_len, local_width), kind)
+    dma = pltpu.SemaphoreType.DMA
+    return pl.pallas_call(
+        functools.partial(layer_kernel, dp_count, tensor_count, slot_count),
+        out_shape=(jax.ShapeDtypeStruct(queries.shape, queries.dtype), arrived, arrived),
+        in_specs=[pl.BlockSpec(memory_space=pltpu.SMEM)] * 3
+        + [pl.BlockSpec(memory_space=pl.ANY)] * 5,
+        out_specs=(pl.BlockSpec(memory_space=pltpu.VMEM),) * 3,
+        scratch_shapes=[
+            pltpu.VMEM((dp_count, step_count, row_count, depth), kind),
+            pltpu.VMEM((2, depth, local_width), kind),
+            pltpu.VMEM((2,) + cache_keys.shape, kind),
+            pltpu.VMEM(queries.shape, kind),
+            pltpu.VMEM((kv_heads, lines, HD), jnp.float32),
+            pltpu.VMEM((kv_heads, lines, cache_len), jnp.float32),
+            pltpu.VMEM((kv_heads, lines, HD), jnp.float32),
+            pltpu.VMEM((kv_heads, lines, HD), jnp.float32),
+            pltpu.VMEM((chips, 2, 2, tokens, local_width), jnp.float32),
+            pltpu.VMEM((chips, 2, tokens, local_width), jnp.float32),
+            pltpu.VMEM((chips, 2, tokens, local_width), jnp.float32),
+            pltpu.VMEM((chips, 2, tokens, local_width), jnp.float32),
+            pltpu.VMEM((2, kv_heads, row_count * PAD, HD), jnp.float32),
+            pltpu.VMEM((2, 2, slot_count, cache_len, local_width), kind),
+            pltpu.VMEM((2, 2, slot_count, cache_len, local_width), kind),
+            pltpu.VMEM((2, slot_count, 2, PAD, local_width), jnp.float32),
+            pltpu.VMEM((2, slot_count, 2, PAD, local_width), jnp.float32),
+            pltpu.VMEM((kv_heads, lines, HD), jnp.float32),
+            dma((5,)),
+            dma((chips, 2)),
+            dma((chips, 2)),
+            dma((tensor_count,)),
+            dma((tensor_count,)),
+            dma((2,)),
+            dma((2,)),
+            dma((chips,)),
+            dma((chips,)),
+            dma((chips,)),
+            dma((chips,)),
+            dma((2,)),
+            dma((2,)),
+        ],
+        compiler_params=pltpu.CompilerParams(
+            collective_id=0, has_side_effects=True, vmem_limit_bytes=60 * 1024 * 1024
+        ),
+        name="layer",
+    )(lengths, finished, row_moves, hidden, queries, projections, cache_keys, cache_values)
+
+
 def solution(mesh):
     in_specs = (
         P(None, "dp", None),
@@ -115,6 +542,15 @@
         P("dp"),
     )
     out_specs = (P(None, "dp", "tensor"), P("dp", None, "tensor"), P("dp", None, "tensor"))
-    return jax.shard_map(
-        per_device, mesh=mesh, in_specs=in_specs, out_specs=out_specs, check_vma=False
-    )
+
+    def whole(*args):
+        fast = fits_kernel(mesh, *args)
+        return jax.shard_map(
+            per_device_kernel if fast else per_device,
+            mesh=mesh,
+            in_specs=in_specs,
+            out_specs=out_specs,
+            check_vma=False,
+        )(*args)
+
+    return whole

time: 157 us -> 70.3 us (0.45)
  waiting for transfers between devices: 76.4 us -> 0 us
  Pallas kernels: 0 us -> 64.7 us
  blocking collectives: 19.1 us -> 0 us
  matrix products: 16.2 us -> 0 us
  between operations: 14.3 us -> 0.65 us
  local copies, waits for them, and re-layouts: 14.7 us -> 4.69 us
  other arithmetic: 8.26 us -> 0 us
  starting transfers between devices: 7.32 us -> 0 us
    all_gather x1 -> x0, waiting for transfers between devices: 70.5 us -> none  [per_device(): portion = lax.all_gather(regrouped, 'dp', axis=1, tiled=True)]
    pallas_call x0 -> x1, Pallas kernels: none -> 64.7 us  [per_device_kernel(): pl.pallas_call(functools.partial(layer_kernel, dp_count, tensor_count, sl...]
    all_to_all x1 -> x0, blocking collectives: 19.1 us -> none  [per_device(): lax.all_to_all(projections, 'tensor', split_axis=2, concat_axis=1, tiled=...]
    dot_general x10 -> x0, matrix products: 16.2 us -> none  [the longest x1 4.29 us: attend(): score_old = jnp.einsum('trkgd,rpkd->trkgp', query_f, cached_k) * inv_root]
    ppermute x4 -> x0, starting transfers between devices: 7.28 us -> none  [shifted(): lax.ppermute(shard, axis, [(i, (i + by) % size) for i in range(size)])]
    reshape x4 -> x0, local copies, waits for them, and re-layouts: 6.89 us -> none  [the longest x1 4.16 us: attend(): old_keys.astype(jnp.float32).reshape(row_count, cache_len, kv_heads, HD)]
    ppermute x4 -> x0, waiting for transfers between devices: 5.8 us -> none  [shifted(): lax.ppermute(shard, axis, [(i, (i + by) % size) for i in range(size)])]
    concatenate x2 -> x0, other arithmetic: 4.13 us -> none  [the longest x1 2.06 us: per_device(): arrived_values = jnp.concatenate([from_before[1], from_after[1]], axis=0)]
  transfers between devices with their start and end apart: 5 -> 0, of which waited for: 3 -> 0; matrix products, arithmetic and copies ran while one was open for 12% -> 0% of each run, Pallas kernels for 0% -> 0%
where the time goes in v1:
time: 70.3 us; the launch traced here: 70.1 us
  Pallas kernels  64.7 us (92%)
  local copies, waits for them, and re-layouts  4.69 us (7%)
    pallas_call x1, Pallas kernels, per_device_kernel(): pl.pallas_call(functools.partial(layer_kernel, dp_count, tensor_count, sl...  64.7 us
    unnamed x5, local copies, waits for them, and re-layouts  4.69 us

profile of v1, /device:TPU:0, one launch (start us, length us, event | category | flops | bytes accessed | tf_op | source)
XLA Modules:
  0.0 70.1 jit_solution(13013613034015090470)
XLA Ops:
  0.6 64.7 %layer.1 = (bf16[4,16,2048]{2,1,0:T(8,128)(2,1)}, bf16[6,256,256]{2,1,0:T(8,128)(2,1)}, bf16[6,256,256]{2,1,0:T(8,128)(2,1)}) custom-call(s32[16]{0:T(128)} %lengths.1, s32[16]{0:T(128)} %finished.1, s32[16]{0:T(128)} %moves.1, bf16[4,16,8192]{2,1,0:T(8,128)(2,1)} %hidden.1, bf16[4,16,2048]{2,1,0:T(8,128)(2,1)} %queries.1, ...), custom_call_target="tpu_custom_call" | custom-call | tf_op jit(solution)/shard_map/layer/pallas_call | solution.py:487
  65.4 0.0 copy-start
  65.4 1.7 %copy.14 = bf16[4,16,2048]{2,1,0:T(8,128)(2,1)} copy(bf16[4,16,2048]{2,1,0:T(8,128)(2,1)} %get-tuple-element.6) | data formatting | bytes 524288
  67.1 2.1 %copy.15 = bf16[6,256,256]{2,1,0:T(8,128)(2,1)} copy(bf16[6,256,256]{2,1,0:T(8,128)(2,1)} %get-tuple-element.7) | data formatting | bytes 1572864
  69.2 0.0 copy-done
  69.2 0.9 %copy.16 = bf16[6,256,256]{2,1,0:T(8,128)(2,1)} copy(bf16[6,256,256]{2,1,0:T(8,128)(2,1)S(1)} %copy-done) | data formatting | bytes 1572864
Async XLA Ops:
  65.4 3.8 %copy-start = (bf16[6,256,256]{2,1,0:T(8,128)(2,1)S(1)}, bf16[6,256,256]{2,1,0:T(8,128)(2,1)}, u32[]{:S(2)}) copy-start(bf16[6,256,256]{2,1,0:T(8,128)(2,1)} %get-tuple-element.8) | copy-start | bytes 2359300

commit v2 on v1

--- a/solution.py
+++ b/solution.py
@@ -9,6 +9,7 @@
 
 HD = 128
 PAD = 8
+RING = 4
 MESH = pl.DeviceIdType.MESH
 
 
@@ -116,12 +117,12 @@
     shard_rows = projections.shape[1] // (dp_count * tensor_count)
     local_width = cache_keys.shape[2] // tensor_count
     return (
-        dp_count % 2 == 0
-        and 4 <= dp_count <= 16
+        dp_count == 2 * RING
         and tensor_count <= 8
         and projections.shape[1] == model_width
         and shard_rows % 128 == 0
         and row_count % 16 == 0
+        and (shard_rows * tensor_count) % 256 == 0
         and local_width % HD == 0
         and step_count < PAD
         and cache_keys.shape[1] % 128 == 0
@@ -141,9 +142,10 @@
     cache_keys,
     cache_values,
     attention,
-    arrived_keys,
-    arrived_values,
+    landed,
+    news_in,
     hid,
+    relay,
     wts,
     cache,
     qry,
@@ -154,16 +156,17 @@
     part,
     mate_part,
     joined,
+    via,
     far_part,
     fresh,
     staged,
-    landed,
     news,
-    news_in,
     out_rows,
     local_sem,
     hid_send,
     hid_recv,
+    relay_send,
+    relay_recv,
     wt_send,
     wt_recv,
     move_send,
@@ -172,6 +175,8 @@
     mate_recv,
     far_send,
     far_recv,
+    via_send,
+    via_recv,
     news_send,
     news_recv,
 ):
@@ -184,6 +189,7 @@
     span = step_count * group
     tokens = step_count * row_count
     chips = dp_count // 2
+    half = depth // 2
     me = lax.axis_index("dp")
     col = lax.axis_index("tensor")
     chip, core = me // 2, me % 2
@@ -224,22 +230,44 @@
         )
     pl.semaphore_wait(barrier, dp_count + tensor_count - 2)
 
-    far_first = sorted(range(1, chips), key=lambda d: -min(d, chips - d))
+    ways = (1, chips - 1)
     hid_copies = []
-    for d in far_first + [0]:
+    for h, d in enumerate(ways):
         for to_core in range(2):
-            if d == 0 and to_core == 1:
-                continue
-            to = ((chip + d) % chips) * 2 + to_core if d else mate
+            to = ((chip + 2 * d) % chips) * 2 + to_core
+            start = pl.multiple_of(to * depth + h * half, 128)
+            copy = remote(
+                hidden.at[:, :, pl.ds(start, half)],
+                relay.at[h, to_core],
+                relay_send.at[h, to_core],
+                relay_recv.at[h, to_core],
+                ((chip + d) % chips) * 2 + core,
+            )
+            copy.start()
+            hid_copies.append(copy)
+    relays_in = list(hid_copies)
+    for to_core in range(2):
+        for h, d in enumerate(ways):
+            to = ((chip + d) % chips) * 2 + to_core
             copy = remote(
                 hidden.at[:, :, pl.ds(pl.multiple_of(to * depth, 128), depth)],
                 hid.at[me],
-                hid_send.at[d, to_core],
-                hid_recv.at[d, core],
+                hid_send.at[h, to_core],
+                hid_recv.at[h, core],
                 to,
             )
             copy.start()
             hid_copies.append(copy)
+    copy = remote(
+        hidden.at[:, :, pl.ds(pl.multiple_of(mate * depth, 128), depth)],
+        hid.at[me],
+        hid_send.at[2, 0],
+        hid_recv.at[2, 0],
+        mate,
+    )
+    copy.start()
+    hid_copies.append(copy)
+    mate_hidden = copy
     wt_copies = []
     for off in range(1, tensor_count):
         to = (col + off) % tensor_count
@@ -299,12 +327,29 @@
                 ].astype(jnp.float32)
     fresh[...] = jnp.zeros_like(fresh)
 
-    move_copies = []
-    for way in range(2):
+    for h, d in enumerate(ways):
+        source = ((chip + chips - d) % chips) * 2 + core
+        for to_core in range(2):
+            relays_in[2 * h + to_core].wait_recv()
+            copy = remote(
+                relay.at[h, to_core],
+                hid.at[source, :, :, h * half : (h + 1) * half],
+                hid_send.at[3 + h, to_core],
+                hid_recv.at[3 + h, core],
+                ((chip + d) % chips) * 2 + to_core,
+            )
+            copy.start()
+            hid_copies.append(copy)
+
+    def move(way, kv):
         to = (me + (1 if way == 0 else dp_count - 1)) % dp_count
-        copy = remote(staged.at[way], landed.at[way], move_send.at[way], move_recv.at[way], to)
+        copy = remote(
+            staged.at[way, kv], landed.at[way, kv], move_send.at[way, kv], move_recv.at[way, kv], to
+        )
         copy.start()
-        move_copies.append(copy)
+        return copy
+
+    move_copies = [move(way, 0) for way in range(2)]
 
     inv_root = HD ** (-0.5)
     masked_out = jnp.float32(-1e30)
@@ -336,21 +381,33 @@
         source = (col + tensor_count - off) % tensor_count
         block = wts.at[:, pl.ds(pl.multiple_of(source * shard_rows, 128), shard_rows), :]
         remote(block, block, wt_send.at[off], wt_recv.at[off], me, source).wait_recv()
-    near_first = [0] + far_first[::-1]
     mate_copies = [None] * chips
-    for d in near_first:
+    for d in (0, 1, chips - 1, 2):
         source_chip = (chip + d) % chips
-        back = (chips - d) % chips
-        for from_core in range(2):
-            if d:
-                source = source_chip * 2 + from_core
-                block = hid.at[source]
+        if d == 0:
+            mate_hidden.wait_recv()
+        elif d == 2:
+            for h in range(2):
+                for from_core in range(2):
+                    block = hid.at[source_chip * 2 + from_core, :, :, h * half : (h + 1) * half]
+                    remote(
+                        block,
+                        block,
+                        hid_send.at[3 + h, from_core],
+                        hid_recv.at[3 + h, from_core],
+                        source_chip * 2 + from_core,
+                    ).wait_recv()
+        else:
+            h = 1 if d == 1 else 0
+            for from_core in range(2):
+                block = hid.at[source_chip * 2 + from_core]
                 remote(
-                    block, block, hid_send.at[back, from_core], hid_recv.at[back, from_core], source
+                    block,
+                    block,
+                    hid_send.at[h, from_core],
+                    hid_recv.at[h, from_core],
+                    source_chip * 2 + from_core,
                 ).wait_recv()
-        if d == 0:
-            block = hid.at[mate]
-            remote(block, block, hid_send.at[0, 0], hid_recv.at[0, 1 - core], mate).wait_recv()
         states = hid[pl.ds(source_chip * 2, 2)].reshape(2 * tokens, depth)
         for kv in range(2):
             product = jnp.dot(states, wts[kv], preferred_element_type=jnp.float32)
@@ -360,26 +417,51 @@
         )
         copy.start()
         mate_copies[d] = copy
+
     far_copies = []
-    for d in near_first[1:] + [0]:
+
+    def send_far(h, kv):
+        copy = remote(
+            joined.at[ways[h], kv],
+            far_part.at[h, kv],
+            far_send.at[h, kv],
+            far_recv.at[h, kv],
+            ((chip + ways[h]) % chips) * 2 + core,
+        )
+        copy.start()
+        far_copies.append(copy)
+
+    def join(d):
         mate_copies[d].wait_recv()
         joined[d] = part[d, core] + mate_part[d]
-        if d:
-            copy = remote(
-                joined.at[d],
-                far_part.at[d],
-                far_send.at[d],
-                far_recv.at[d],
-                ((chip + d) % chips) * 2 + core,
-            )
-            copy.start()
-            far_copies.append(copy)
+
+    join(1)
+    send_far(0, 1)
+    join(chips - 1)
+    send_far(1, 0)
+    join(0)
+    join(2)
+    via_copies = []
+    for h in range(2):
+        copy = remote(
+            joined.at[2, h],
+            via.at[h],
+            via_send.at[h],
+            via_recv.at[h],
+            ((chip + ways[h]) % chips) * 2 + core,
+        )
+        copy.start()
+        via_copies.append(copy)
+    for h in range(2):
+        via_copies[h].wait_recv()
+        joined[ways[h], h] += via[h]
+        send_far(h, h)
+    move_copies += [move(way, 1) for way in range(2)]
     for copy in far_copies:
         copy.wait_recv()
     for kv in range(2):
         total = joined[0, kv]
-        for d in range(1, chips):
-            total = total + far_part[d, kv]
+        total = total + far_part[0, kv] + far_part[1, kv]
         total = total.astype(jnp.bfloat16).astype(jnp.float32)
         for k in range(kv_heads):
             for t in range(step_count):
@@ -452,19 +534,22 @@
 
     for copy in move_copies + news_copies:
         copy.wait_recv()
+    for copy in hid_copies + wt_copies + move_copies + mate_copies + via_copies + far_copies + news_copies:
+        copy.wait_send()
+
+
+def merge_kernel(raw, landed, news, attention, arrived_keys, arrived_values):
+    step_count = raw.shape[0]
+    attention[...] = raw[...]
+    cache_len, local_width = arrived_keys.shape[1:]
     line = lax.broadcasted_iota(jnp.int32, (cache_len, local_width), 0).astype(jnp.float32)
-    for way in range(2):
-        for s in range(slot_count):
-            for kv, arrived in enumerate((arrived_keys, arrived_values)):
-                rows = news_in[way, s, kv]
-                ahead = line - rows[step_count : step_count + 1]
-                block = landed[way, kv, s].astype(jnp.float32)
-                for t in range(step_count):
-                    block = jnp.where(ahead == t, rows[t : t + 1], block)
-                arrived[way * slot_count + s] = block.astype(arrived.dtype)
-
-    for copy in hid_copies + wt_copies + move_copies + mate_copies + far_copies + news_copies:
-        copy.wait_send()
+    for kv, arrived in enumerate((arrived_keys, arrived_values)):
+        rows = news[0, 0, kv]
+        ahead = line - rows[step_count : step_count + 1]
+        block = landed[0, kv, 0].astype(jnp.float32)
+        for t in range(step_count):
+            block = jnp.where(ahead == t, rows[t : t + 1], block)
+        arrived[0] = block.astype(arrived.dtype)
 
 
 def per_device_kernel(
@@ -484,14 +569,23 @@
     lines = row_count * span
     arrived = jax.ShapeDtypeStruct((2 * slot_count, cache_len, local_width), kind)
     dma = pltpu.SemaphoreType.DMA
-    return pl.pallas_call(
+    raw, landed, news = pl.pallas_call(
         functools.partial(layer_kernel, dp_count, tensor_count, slot_count),
-        out_shape=(jax.ShapeDtypeStruct(queries.shape, queries.dtype), arrived, arrived),
+        out_shape=(
+            jax.ShapeDtypeStruct(queries.shape, queries.dtype),
+            jax.ShapeDtypeStruct((2, 2, slot_count, cache_len, local_width), kind),
+            jax.ShapeDtypeStruct((2, slot_count, 2, PAD, local_width), jnp.float32),
+        ),
         in_specs=[pl.BlockSpec(memory_space=pltpu.SMEM)] * 3
         + [pl.BlockSpec(memory_space=pl.ANY)] * 5,
-        out_specs=(pl.BlockSpec(memory_space=pltpu.VMEM),) * 3,
+        out_specs=(
+            pl.BlockSpec(memory_space=pltpu.VMEM),
+            pl.BlockSpec(memory_space=pl.ANY),
+            pl.BlockSpec(memory_space=pl.ANY),
+        ),
         scratch_shapes=[
             pltpu.VMEM((dp_count, step_count, row_count, depth), kind),
+            pltpu.VMEM((2, 2, step_count, row_count, depth // 2), kind),
             pltpu.VMEM((2, depth, local_width), kind),
             pltpu.VMEM((2,) + cache_keys.shape, kind),
             pltpu.VMEM(queries.shape, kind),
@@ -502,24 +596,27 @@
             pltpu.VMEM((chips, 2, 2, tokens, local_width), jnp.float32),
             pltpu.VMEM((chips, 2, tokens, local_width), jnp.float32),
             pltpu.VMEM((chips, 2, tokens, local_width), jnp.float32),
-            pltpu.VMEM((chips, 2, tokens, local_width), jnp.float32),
+            pltpu.VMEM((2, tokens, local_width), jnp.float32),
+            pltpu.VMEM((2, 2, tokens, local_width), jnp.float32),
             pltpu.VMEM((2, kv_heads, row_count * PAD, HD), jnp.float32),
             pltpu.VMEM((2, 2, slot_count, cache_len, local_width), kind),
-            pltpu.VMEM((2, 2, slot_count, cache_len, local_width), kind),
-            pltpu.VMEM((2, slot_count, 2, PAD, local_width), jnp.float32),
             pltpu.VMEM((2, slot_count, 2, PAD, local_width), jnp.float32),
             pltpu.VMEM((kv_heads, lines, HD), jnp.float32),
             dma((5,)),
-            dma((chips, 2)),
-            dma((chips, 2)),
+            dma((5, 2)),
+            dma((5, 2)),
+            dma((2, 2)),
+            dma((2, 2)),
             dma((tensor_count,)),
             dma((tensor_count,)),
+            dma((2, 2)),
+            dma((2, 2)),
+            dma((chips,)),
+            dma((chips,)),
+            dma((2, 2)),
+            dma((2, 2)),
             dma((2,)),
             dma((2,)),
-            dma((chips,)),
-            dma((chips,)),
-            dma((chips,)),
-            dma((chips,)),
             dma((2,)),
             dma((2,)),
         ],
@@ -528,6 +625,25 @@
         ),
         name="layer",
     )(lengths, finished, row_moves, hidden, queries, projections, cache_keys, cache_values)
+    whole = pl.BlockSpec(queries.shape, lambda n: (0, 0, 0))
+    slot = pl.BlockSpec((1, cache_len, local_width), lambda n: (n, 0, 0))
+    return pl.pallas_call(
+        merge_kernel,
+        grid=(2 * slot_count,),
+        out_shape=(jax.ShapeDtypeStruct(queries.shape, queries.dtype), arrived, arrived),
+        in_specs=[
+            whole,
+            pl.BlockSpec(
+                (1, 2, 1, cache_len, local_width),
+                lambda n: (n // slot_count, 0, n % slot_count, 0, 0),
+            ),
+            pl.BlockSpec(
+                (1, 1, 2, PAD, local_width), lambda n: (n // slot_count, n % slot_count, 0, 0, 0)
+            ),
+        ],
+        out_specs=(whole, slot, slot),
+        name="merge",
+    )(raw, landed, news)
 
 
 def solution(mesh):

time: 70.3 us -> 65.1 us (0.926)
  local copies, waits for them, and re-layouts: 4.69 us -> 0 us
    pallas_call x1, Pallas kernels: 64.7 us -> 59.2 us  [per_device_kernel(): pl.pallas_call(functools.partial(layer_kernel, dp_count, tensor_count, sl...]
    pallas_call x0 -> x1, Pallas kernels: none -> 5.01 us  [per_device_kernel(): pl.pallas_call(merge_kernel, grid=(2 * slot_count,), out_shape=(jax.Shape...]
    unnamed x5 -> x0, local copies, waits for them, and re-layouts: 4.69 us -> none
where the time goes in v2:
time: 65.1 us; the launch traced here: 64.8 us
  Pallas kernels  64.2 us (99%)
    pallas_call x1, Pallas kernels, per_device_kernel(): pl.pallas_call(functools.partial(layer_kernel, dp_count, tensor_count, sl...  59.2 us
    pallas_call x1, Pallas kernels, per_device_kernel(): pl.pallas_call(merge_kernel, grid=(2 * slot_count,), out_shape=(jax.Shape...  5.01 us

profile of v2, /device:TPU:0, one launch (start us, length us, event | category | flops | bytes accessed | tf_op | source)
XLA Modules:
  0.0 64.8 jit_solution(11497823693249922672)
XLA Ops:
  0.6 59.2 %layer.1 = (bf16[4,16,2048]{2,1,0:T(8,128)(2,1)}, bf16[2,2,3,256,256]{4,3,2,1,0:T(8,128)(2,1)}, f32[2,3,2,8,256]{4,3,2,1,0:T(8,128)}) custom-call(s32[16]{0:T(128)} %lengths.1, s32[16]{0:T(128)} %finished.1, s32[16]{0:T(128)} %moves.1, bf16[4,16,8192]{2,1,0:T(8,128)(2,1)} %hidden.1, bf16[4,16,2048]{2,1,0:T(8,128)(2,1)} %queries.1, ...), custom_call_target="tpu_custom_call" | custom-call | tf_op jit(solution)/shard_map/layer/pallas_call | solution.py:572
  59.8 5.0 %merge.1 = (bf16[4,16,2048]{2,1,0:T(8,128)(2,1)}, bf16[6,256,256]{2,1,0:T(8,128)(2,1)}, bf16[6,256,256]{2,1,0:T(8,128)(2,1)}) custom-call(bf16[4,16,2048]{2,1,0:T(8,128)(2,1)} %get-tuple-element.6.raw, bf16[2,2,3,256,256]{4,3,2,1,0:T(8,128)(2,1)} %get-tuple-element.7.landed, f32[2,3,2,8,256]{4,3,2,1,0:T(8,128)} %get-tuple-element.8.news), custom_call_target="tpu_custom_call" | custom-call | tf_op jit(solution)/shard_map/merge/pallas_call | solution.py:630

commit v3 on v1

--- a/solution.py
+++ b/solution.py
@@ -141,8 +141,8 @@
     cache_keys,
     cache_values,
     attention,
-    arrived_keys,
-    arrived_values,
+    landed,
+    news_in,
     hid,
     wts,
     cache,
@@ -157,13 +157,13 @@
     far_part,
     fresh,
     staged,
-    landed,
     news,
-    news_in,
     out_rows,
     local_sem,
     hid_send,
     hid_recv,
+    share_send,
+    share_recv,
     wt_send,
     wt_recv,
     move_send,
@@ -202,15 +202,20 @@
     load_keys = pltpu.make_async_copy(cache_keys, cache.at[0], local_sem.at[0])
     load_values = pltpu.make_async_copy(cache_values, cache.at[1], local_sem.at[1])
     load_queries = pltpu.make_async_copy(queries, qry, local_sem.at[2])
-    own_hidden = pltpu.make_async_copy(
-        hidden.at[:, :, pl.ds(pl.multiple_of(me * depth, 128), depth)], hid.at[me], local_sem.at[3]
-    )
+    own_hidden = [
+        pltpu.make_async_copy(
+            hidden.at[:, :, pl.ds(pl.multiple_of(me * depth + n * shard_rows, 128), shard_rows)],
+            hid.at[me, n],
+            local_sem.at[5 + n],
+        )
+        for n in range(tensor_count)
+    ]
     own_weights = pltpu.make_async_copy(
         projections.at[:, :, pl.ds(pl.multiple_of(col * local_width, 128), local_width)],
-        wts.at[:, pl.ds(pl.multiple_of(col * shard_rows, 128), shard_rows), :],
+        wts.at[col],
         local_sem.at[4],
     )
-    for copy in (load_keys, load_values, load_queries, own_hidden, own_weights):
+    for copy in (load_keys, load_values, load_queries, own_weights, *own_hidden):
         copy.start()
 
     barrier = pltpu.get_barrier_semaphore()
@@ -226,26 +231,37 @@
 
     far_first = sorted(range(1, chips), key=lambda d: -min(d, chips - d))
     hid_copies = []
-    for d in far_first + [0]:
+    for d in far_first:
         for to_core in range(2):
-            if d == 0 and to_core == 1:
-                continue
-            to = ((chip + d) % chips) * 2 + to_core if d else mate
+            to = ((chip + d) % chips) * 2 + to_core
+            start = pl.multiple_of(to * depth + col * shard_rows, 128)
             copy = remote(
-                hidden.at[:, :, pl.ds(pl.multiple_of(to * depth, 128), depth)],
-                hid.at[me],
+                hidden.at[:, :, pl.ds(start, shard_rows)],
+                hid.at[me, col],
                 hid_send.at[d, to_core],
                 hid_recv.at[d, core],
                 to,
             )
             copy.start()
             hid_copies.append(copy)
+    mate_hidden = [
+        remote(
+            hidden.at[:, :, pl.ds(pl.multiple_of(mate * depth + n * shard_rows, 128), shard_rows)],
+            hid.at[me, n],
+            share_send.at[0, n],
+            share_recv.at[0, n],
+            mate,
+        )
+        for n in range(tensor_count)
+    ]
+    for copy in mate_hidden:
+        copy.start()
     wt_copies = []
     for off in range(1, tensor_count):
         to = (col + off) % tensor_count
         copy = remote(
             projections.at[:, :, pl.ds(pl.multiple_of(to * local_width, 128), local_width)],
-            wts.at[:, pl.ds(pl.multiple_of(col * shard_rows, 128), shard_rows), :],
+            wts.at[col],
             wt_send.at[off],
             wt_recv.at[off],
             me,
@@ -299,12 +315,38 @@
                 ].astype(jnp.float32)
     fresh[...] = jnp.zeros_like(fresh)
 
-    move_copies = []
-    for way in range(2):
+    near_first = far_first[::-1]
+    for d in near_first:
+        source_chip = (chip + d) % chips
+        back = chips - d
+        for from_core in range(2):
+            source = source_chip * 2 + from_core
+            block = hid.at[source, col]
+            remote(
+                block, block, hid_send.at[back, from_core], hid_recv.at[back, from_core], source
+            ).wait_recv()
+        block = hid.at[pl.ds(source_chip * 2, 2), col]
+        for off in range(1, tensor_count):
+            copy = remote(
+                block,
+                block,
+                share_send.at[d, off],
+                share_recv.at[d, off],
+                me,
+                (col + off) % tensor_count,
+            )
+            copy.start()
+            hid_copies.append(copy)
+
+    def move(way, kv):
         to = (me + (1 if way == 0 else dp_count - 1)) % dp_count
-        copy = remote(staged.at[way], landed.at[way], move_send.at[way], move_recv.at[way], to)
+        copy = remote(
+            staged.at[way, kv], landed.at[way, kv], move_send.at[way, kv], move_recv.at[way, kv], to
+        )
         copy.start()
-        move_copies.append(copy)
+        return copy
+
+    move_copies = [move(way, kv) for kv in range(2) for way in range(2)]
 
     inv_root = HD ** (-0.5)
     masked_out = jnp.float32(-1e30)
@@ -330,38 +372,40 @@
 
     lax.fori_loop(0, row_count, old_scores, 0, unroll=4)
 
-    own_hidden.wait()
+    for copy in own_hidden:
+        copy.wait()
     own_weights.wait()
     for off in range(1, tensor_count):
         source = (col + tensor_count - off) % tensor_count
-        block = wts.at[:, pl.ds(pl.multiple_of(source * shard_rows, 128), shard_rows), :]
+        block = wts.at[source]
         remote(block, block, wt_send.at[off], wt_recv.at[off], me, source).wait_recv()
-    near_first = [0] + far_first[::-1]
     mate_copies = [None] * chips
-    for d in near_first:
+    for d in [0] + near_first:
         source_chip = (chip + d) % chips
-        back = (chips - d) % chips
-        for from_core in range(2):
+        if d == 0:
+            for copy in mate_hidden:
+                copy.wait_recv()
+        for off in range(1, tensor_count):
             if d:
-                source = source_chip * 2 + from_core
-                block = hid.at[source]
+                source_col = (col + tensor_count - off) % tensor_count
+                block = hid.at[pl.ds(source_chip * 2, 2), source_col]
                 remote(
-                    block, block, hid_send.at[back, from_core], hid_recv.at[back, from_core], source
+                    block, block, share_send.at[d, off], share_recv.at[d, off], me, source_col
                 ).wait_recv()
-        if d == 0:
-            block = hid.at[mate]
-            remote(block, block, hid_send.at[0, 0], hid_recv.at[0, 1 - core], mate).wait_recv()
-        states = hid[pl.ds(source_chip * 2, 2)].reshape(2 * tokens, depth)
         for kv in range(2):
-            product = jnp.dot(states, wts[kv], preferred_element_type=jnp.float32)
+            product = jnp.zeros((2 * tokens, local_width), jnp.float32)
+            for n in range(tensor_count):
+                states = hid[pl.ds(source_chip * 2, 2), n].reshape(2 * tokens, shard_rows)
+                product += jnp.dot(states, wts[n, kv], preferred_element_type=jnp.float32)
             part[d, :, kv] = product.reshape(2, tokens, local_width)
         copy = remote(
             part.at[d, 1 - core], mate_part.at[d], mate_send.at[d], mate_recv.at[d], mate
         )
         copy.start()
         mate_copies[d] = copy
+
     far_copies = []
-    for d in near_first[1:] + [0]:
+    for d in near_first + [0]:
         mate_copies[d].wait_recv()
         joined[d] = part[d, core] + mate_part[d]
         if d:
@@ -452,19 +496,22 @@
 
     for copy in move_copies + news_copies:
         copy.wait_recv()
+    for copy in hid_copies + mate_hidden + wt_copies + move_copies + mate_copies + far_copies + news_copies:
+        copy.wait_send()
+
+
+def merge_kernel(raw, landed, news, attention, arrived_keys, arrived_values):
+    step_count = raw.shape[0]
+    attention[...] = raw[...]
+    cache_len, local_width = arrived_keys.shape[1:]
     line = lax.broadcasted_iota(jnp.int32, (cache_len, local_width), 0).astype(jnp.float32)
-    for way in range(2):
-        for s in range(slot_count):
-            for kv, arrived in enumerate((arrived_keys, arrived_values)):
-                rows = news_in[way, s, kv]
-                ahead = line - rows[step_count : step_count + 1]
-                block = landed[way, kv, s].astype(jnp.float32)
-                for t in range(step_count):
-                    block = jnp.where(ahead == t, rows[t : t + 1], block)
-                arrived[way * slot_count + s] = block.astype(arrived.dtype)
-
-    for copy in hid_copies + wt_copies + move_copies + mate_copies + far_copies + news_copies:
-        copy.wait_send()
+    for kv, arrived in enumerate((arrived_keys, arrived_values)):
+        rows = news[0, 0, kv]
+        ahead = line - rows[step_count : step_count + 1]
+        block = landed[0, kv, 0].astype(jnp.float32)
+        for t in range(step_count):
+            block = jnp.where(ahead == t, rows[t : t + 1], block)
+        arrived[0] = block.astype(arrived.dtype)
 
 
 def per_device_kernel(
@@ -475,7 +522,7 @@
     step_count, row_count, _ = hidden.shape
     _, cache_len, local_width = cache_keys.shape
     slot_count = max(2, row_count // 5)
-    depth = projections.shape[1] * tensor_count
+    shard_rows = projections.shape[1]
     kv_heads = local_width // HD
     span = step_count * (queries.shape[2] // local_width)
     tokens = step_count * row_count
@@ -484,15 +531,23 @@
     lines = row_count * span
     arrived = jax.ShapeDtypeStruct((2 * slot_count, cache_len, local_width), kind)
     dma = pltpu.SemaphoreType.DMA
-    return pl.pallas_call(
+    raw, landed, news = pl.pallas_call(
         functools.partial(layer_kernel, dp_count, tensor_count, slot_count),
-        out_shape=(jax.ShapeDtypeStruct(queries.shape, queries.dtype), arrived, arrived),
+        out_shape=(
+            jax.ShapeDtypeStruct(queries.shape, queries.dtype),
+            jax.ShapeDtypeStruct((2, 2, slot_count, cache_len, local_width), kind),
+            jax.ShapeDtypeStruct((2, slot_count, 2, PAD, local_width), jnp.float32),
+        ),
         in_specs=[pl.BlockSpec(memory_space=pltpu.SMEM)] * 3
         + [pl.BlockSpec(memory_space=pl.ANY)] * 5,
-        out_specs=(pl.BlockSpec(memory_space=pltpu.VMEM),) * 3,
+        out_specs=(
+            pl.BlockSpec(memory_space=pltpu.VMEM),
+            pl.BlockSpec(memory_space=pl.ANY),
+            pl.BlockSpec(memory_space=pl.ANY),
+        ),
         scratch_shapes=[
-            pltpu.VMEM((dp_count, step_count, row_count, depth), kind),
-            pltpu.VMEM((2, depth, local_width), kind),
+            pltpu.VMEM((dp_count, tensor_count, step_count, row_count, shard_rows), kind),
+            pltpu.VMEM((tensor_count, 2, shard_rows, local_width), kind),
             pltpu.VMEM((2,) + cache_keys.shape, kind),
             pltpu.VMEM(queries.shape, kind),
             pltpu.VMEM((kv_heads, lines, HD), jnp.float32),
@@ -505,17 +560,17 @@
             pltpu.VMEM((chips, 2, tokens, local_width), jnp.float32),
             pltpu.VMEM((2, kv_heads, row_count * PAD, HD), jnp.float32),
             pltpu.VMEM((2, 2, slot_count, cache_len, local_width), kind),
-            pltpu.VMEM((2, 2, slot_count, cache_len, local_width), kind),
-            pltpu.VMEM((2, slot_count, 2, PAD, local_width), jnp.float32),
             pltpu.VMEM((2, slot_count, 2, PAD, local_width), jnp.float32),
             pltpu.VMEM((kv_heads, lines, HD), jnp.float32),
-            dma((5,)),
+            dma((5 + tensor_count,)),
             dma((chips, 2)),
             dma((chips, 2)),
+            dma((chips, tensor_count)),
+            dma((chips, tensor_count)),
             dma((tensor_count,)),
             dma((tensor_count,)),
-            dma((2,)),
-            dma((2,)),
+            dma((2, 2)),
+            dma((2, 2)),
             dma((chips,)),
             dma((chips,)),
             dma((chips,)),
@@ -528,6 +583,25 @@
         ),
         name="layer",
     )(lengths, finished, row_moves, hidden, queries, projections, cache_keys, cache_values)
+    whole = pl.BlockSpec(queries.shape, lambda n: (0, 0, 0))
+    slot = pl.BlockSpec((1, cache_len, local_width), lambda n: (n, 0, 0))
+    return pl.pallas_call(
+        merge_kernel,
+        grid=(2 * slot_count,),
+        out_shape=(jax.ShapeDtypeStruct(queries.shape, queries.dtype), arrived, arrived),
+        in_specs=[
+            whole,
+            pl.BlockSpec(
+                (1, 2, 1, cache_len, local_width),
+                lambda n: (n // slot_count, 0, n % slot_count, 0, 0),
+            ),
+            pl.BlockSpec(
+                (1, 1, 2, PAD, local_width), lambda n: (n // slot_count, n % slot_count, 0, 0, 0)
+            ),
+        ],
+        out_specs=(whole, slot, slot),
+        name="merge",
+    )(raw, landed, news)
 
 
 def solution(mesh):

time: 70.3 us -> 54.8 us (0.78)
  Pallas kernels: 64.7 us -> 54 us
  local copies, waits for them, and re-layouts: 4.69 us -> 0 us
    pallas_call x1, Pallas kernels: 64.7 us -> 49 us  [per_device_kernel(): pl.pallas_call(functools.partial(layer_kernel, dp_count, tensor_count, sl...]
    pallas_call x0 -> x1, Pallas kernels: none -> 5.01 us  [per_device_kernel(): pl.pallas_call(merge_kernel, grid=(2 * slot_count,), out_shape=(jax.Shape...]
    unnamed x5 -> x0, local copies, waits for them, and re-layouts: 4.69 us -> none
where the time goes in v3:
time: 54.8 us; the launch traced here: 54.6 us
  Pallas kernels  54 us (99%)
  between operations  0.64 us (1%)
    pallas_call x1, Pallas kernels, per_device_kernel(): pl.pallas_call(functools.partial(layer_kernel, dp_count, tensor_count, sl...  49 us
    pallas_call x1, Pallas kernels, per_device_kernel(): pl.pallas_call(merge_kernel, grid=(2 * slot_count,), out_shape=(jax.Shape...  5.01 us

profile of v3, /device:TPU:0, one launch (start us, length us, event | category | flops | bytes accessed | tf_op | source)
XLA Modules:
  0.0 54.6 jit_solution(6626292113336698958)
XLA Ops:
  0.6 49.0 %layer.1 = (bf16[4,16,2048]{2,1,0:T(8,128)(2,1)}, bf16[2,2,3,256,256]{4,3,2,1,0:T(8,128)(2,1)}, f32[2,3,2,8,256]{4,3,2,1,0:T(8,128)}) custom-call(s32[16]{0:T(128)} %lengths.1, s32[16]{0:T(128)} %finished.1, s32[16]{0:T(128)} %moves.1, bf16[4,16,8192]{2,1,0:T(8,128)(2,1)} %hidden.1, bf16[4,16,2048]{2,1,0:T(8,128)(2,1)} %queries.1, ...), custom_call_target="tpu_custom_call" | custom-call | tf_op jit(solution)/shard_map/layer/pallas_call | solution.py:534
  49.6 5.0 %merge.1 = (bf16[4,16,2048]{2,1,0:T(8,128)(2,1)}, bf16[6,256,256]{2,1,0:T(8,128)(2,1)}, bf16[6,256,256]{2,1,0:T(8,128)(2,1)}) custom-call(bf16[4,16,2048]{2,1,0:T(8,128)(2,1)} %get-tuple-element.6.raw, bf16[2,2,3,256,256]{4,3,2,1,0:T(8,128)(2,1)} %get-tuple-element.7.landed, f32[2,3,2,8,256]{4,3,2,1,0:T(8,128)} %get-tuple-element.8.news), custom_call_target="tpu_custom_call" | custom-call | tf_op jit(solution)/shard_map/merge/pallas_call | solution.py:588

commit v4 on v3

--- a/solution.py
+++ b/solution.py
@@ -154,6 +154,7 @@
     part,
     mate_part,
     joined,
+    far_out,
     far_part,
     fresh,
     staged,
@@ -380,7 +381,27 @@
         block = wts.at[source]
         remote(block, block, wt_send.at[off], wt_recv.at[off], me, source).wait_recv()
     mate_copies = [None] * chips
-    for d in [0] + near_first:
+    far_copies = []
+
+    def join(d):
+        mate_copies[d].wait_recv()
+        total = part[d, core] + mate_part[d]
+        if not d:
+            joined[...] = total
+            return
+        far_out[d] = total.astype(far_out.dtype)
+        copy = remote(
+            far_out.at[d],
+            far_part.at[d],
+            far_send.at[d],
+            far_recv.at[d],
+            ((chip + d) % chips) * 2 + core,
+        )
+        copy.start()
+        far_copies.append(copy)
+
+    order = near_first + [0]
+    for at, d in enumerate(order):
         source_chip = (chip + d) % chips
         if d == 0:
             for copy in mate_hidden:
@@ -403,27 +424,16 @@
         )
         copy.start()
         mate_copies[d] = copy
-
-    far_copies = []
-    for d in near_first + [0]:
-        mate_copies[d].wait_recv()
-        joined[d] = part[d, core] + mate_part[d]
-        if d:
-            copy = remote(
-                joined.at[d],
-                far_part.at[d],
-                far_send.at[d],
-                far_recv.at[d],
-                ((chip + d) % chips) * 2 + core,
-            )
-            copy.start()
-            far_copies.append(copy)
+        if at:
+            join(order[at - 1])
+
+    join(0)
     for copy in far_copies:
         copy.wait_recv()
     for kv in range(2):
-        total = joined[0, kv]
+        total = joined[kv]
         for d in range(1, chips):
-            total = total + far_part[d, kv]
+            total = total + far_part[d, kv].astype(jnp.float32)
         total = total.astype(jnp.bfloat16).astype(jnp.float32)
         for k in range(kv_heads):
             for t in range(step_count):
@@ -556,8 +566,9 @@
             pltpu.VMEM((kv_heads, lines, HD), jnp.float32),
             pltpu.VMEM((chips, 2, 2, tokens, local_width), jnp.float32),
             pltpu.VMEM((chips, 2, tokens, local_width), jnp.float32),
-            pltpu.VMEM((chips, 2, tokens, local_width), jnp.float32),
-            pltpu.VMEM((chips, 2, tokens, local_width), jnp.float32),
+            pltpu.VMEM((2, tokens, local_width), jnp.float32),
+            pltpu.VMEM((chips, 2, tokens, local_width), kind),
+            pltpu.VMEM((chips, 2, tokens, local_width), kind),
             pltpu.VMEM((2, kv_heads, row_count * PAD, HD), jnp.float32),
             pltpu.VMEM((2, 2, slot_count, cache_len, local_width), kind),
             pltpu.VMEM((2, slot_count, 2, PAD, local_width), jnp.float32),

time: 54.8 us -> 49.1 us (0.90)
  Pallas kernels: 54 us -> 48.2 us
    pallas_call x1, Pallas kernels: 49 us -> 43.2 us  [per_device_kernel(): pl.pallas_call(functools.partial(layer_kernel, dp_count, tensor_count, sl...]
where the time goes in v4:
time: 49.1 us; the launch traced here: 48.8 us
  Pallas kernels  48.2 us (98%)
  between operations  0.64 us (1%)
    pallas_call x1, Pallas kernels, per_device_kernel(): pl.pallas_call(functools.partial(layer_kernel, dp_count, tensor_count, sl...  43.2 us
    pallas_call x1, Pallas kernels, per_device_kernel(): pl.pallas_call(merge_kernel, grid=(2 * slot_count,), out_shape=(jax.Shape...  5.01 us

profile of v4, /device:TPU:0, one launch (start us, length us, event | category | flops | bytes accessed | tf_op | source)
XLA Modules:
  0.0 48.8 jit_solution(11266405804430785912)
XLA Ops:
  0.6 43.2 %layer.1 = (bf16[4,16,2048]{2,1,0:T(8,128)(2,1)}, bf16[2,2,3,256,256]{4,3,2,1,0:T(8,128)(2,1)}, f32[2,3,2,8,256]{4,3,2,1,0:T(8,128)}) custom-call(s32[16]{0:T(128)} %lengths.1, s32[16]{0:T(128)} %finished.1, s32[16]{0:T(128)} %moves.1, bf16[4,16,8192]{2,1,0:T(8,128)(2,1)} %hidden.1, bf16[4,16,2048]{2,1,0:T(8,128)(2,1)} %queries.1, ...), custom_call_target="tpu_custom_call" | custom-call | tf_op jit(solution)/shard_map/layer/pallas_call | solution.py:544
  43.8 5.0 %merge.1 = (bf16[4,16,2048]{2,1,0:T(8,128)(2,1)}, bf16[6,256,256]{2,1,0:T(8,128)(2,1)}, bf16[6,256,256]{2,1,0:T(8,128)(2,1)}) custom-call(bf16[4,16,2048]{2,1,0:T(8,128)(2,1)} %get-tuple-element.6.raw, bf16[2,2,3,256,256]{4,3,2,1,0:T(8,128)(2,1)} %get-tuple-element.7.landed, f32[2,3,2,8,256]{4,3,2,1,0:T(8,128)} %get-tuple-element.8.news), custom_call_target="tpu_custom_call" | custom-call | tf_op jit(solution)/shard_map/merge/pallas_call | solution.py:599

commit v5 on v4

--- a/solution.py
+++ b/solution.py
@@ -567,8 +567,8 @@
             pltpu.VMEM((chips, 2, 2, tokens, local_width), jnp.float32),
             pltpu.VMEM((chips, 2, tokens, local_width), jnp.float32),
             pltpu.VMEM((2, tokens, local_width), jnp.float32),
-            pltpu.VMEM((chips, 2, tokens, local_width), kind),
-            pltpu.VMEM((chips, 2, tokens, local_width), kind),
+            pltpu.VMEM((chips, 2, tokens, local_width), jnp.float32),
+            pltpu.VMEM((chips, 2, tokens, local_width), jnp.float32),
             pltpu.VMEM((2, kv_heads, row_count * PAD, HD), jnp.float32),
             pltpu.VMEM((2, 2, slot_count, cache_len, local_width), kind),
             pltpu.VMEM((2, slot_count, 2, PAD, local_width), jnp.float32),

time: 49.1 us -> 54.8 us (1.12)
  Pallas kernels: 48.2 us -> 54 us
    pallas_call x1, Pallas kernels: 43.2 us -> 48.9 us  [per_device_kernel(): pl.pallas_call(functools.partial(layer_kernel, dp_count, tensor_count, sl...]
where the time goes in v5:
time: 54.8 us; the launch traced here: 54.6 us
  Pallas kernels  54 us (99%)
  between operations  0.64 us (1%)
    pallas_call x1, Pallas kernels, per_device_kernel(): pl.pallas_call(functools.partial(layer_kernel, dp_count, tensor_count, sl...  48.9 us
    pallas_call x1, Pallas kernels, per_device_kernel(): pl.pallas_call(merge_kernel, grid=(2 * slot_count,), out_shape=(jax.Shape...  5.01 us

profile of v5, /device:TPU:0, one launch (start us, length us, event | category | flops | bytes accessed | tf_op | source)
XLA Modules:
  0.0 54.6 jit_solution(6150472500205332236)
XLA Ops:
  0.6 48.9 %layer.1 = (bf16[4,16,2048]{2,1,0:T(8,128)(2,1)}, bf16[2,2,3,256,256]{4,3,2,1,0:T(8,128)(2,1)}, f32[2,3,2,8,256]{4,3,2,1,0:T(8,128)}) custom-call(s32[16]{0:T(128)} %lengths.1, s32[16]{0:T(128)} %finished.1, s32[16]{0:T(128)} %moves.1, bf16[4,16,8192]{2,1,0:T(8,128)(2,1)} %hidden.1, bf16[4,16,2048]{2,1,0:T(8,128)(2,1)} %queries.1, ...), custom_call_target="tpu_custom_call" | custom-call | tf_op jit(solution)/shard_map/layer/pallas_call | solution.py:544
  49.6 5.0 %merge.1 = (bf16[4,16,2048]{2,1,0:T(8,128)(2,1)}, bf16[6,256,256]{2,1,0:T(8,128)(2,1)}, bf16[6,256,256]{2,1,0:T(8,128)(2,1)}) custom-call(bf16[4,16,2048]{2,1,0:T(8,128)(2,1)} %get-tuple-element.6.raw, bf16[2,2,3,256,256]{4,3,2,1,0:T(8,128)(2,1)} %get-tuple-element.7.landed, f32[2,3,2,8,256]{4,3,2,1,0:T(8,128)} %get-tuple-element.8.news), custom_call_target="tpu_custom_call" | custom-call | tf_op jit(solution)/shard_map/merge/pallas_call | solution.py:599
